TPU v7x, 32 devices: a whole 2x2x4 slice. The times are simulated.
32 devices in a mesh: field: 16 (over z, y, core), probe: 2 (over x).
Axes of the slice: x: 2, y: 2, z: 4, core: 2. Of those that a mesh axis runs over, the one named last changes fastest.
Arguments:
- probes: bfloat16 [16, 4, 512, 256], P('probe', None, 'field'), may hold values from -6 to 6
- matern_shift: float32 [4, 512, 256], P(None, 'field'), may hold values from 0.25 to 2
- diffusivity: float32 [4, 512, 256], P(None, 'field'), may hold values from 0.03 to 0.1
- sensor_count: int32 [16], P('field'), may hold values from 1 to 256, 2560 in all
- sensor_cell: int32 [16, 256], P('field'), may hold values from 0 to 32767
- sensor_owner: int32 [16, 256, 1], P('field'), may hold values from 0 to 15; in each aligned block of 256 rows (0 to 255, 256 to 511, ..., all dimensions but the last counted through in order) at most 24 rows name the same one
- design_logit: float32 [16, 16, 24], P('field'), may hold values from -6 to 6
- noise_precision: float32 [16, 16, 24], P('field'), may hold values from 1 to 8
Outputs:
- hessian_probes: float32 [16, 4, 512, 256], P('probe', None, 'field')
- tiles: float32 [16, 16], P('probe')
- weight_grad: float32 [16, 16, 24], P('field')
Inputs may be any that keep to these rules, and one draw needn't show every extreme that they name: `sensor_count`: the counts sum to 2560 and the largest is 256. `sensor_cell`: flat cell index within the block; several slots may share a cell. `sensor_owner`: among the 256 slots of one block, live or not, no owner is named by more than 24 slots, a bound that some block reaches.
All inputs are finite; a program needn't handle non-finite values. No bound on the sum of `sensor_count` on one device may be relied on, other than what follows from the above.
Results may differ from a plain program's by a relative error of at most 0.00035.
Values may be sent and summed in bfloat16 or wider, within the bound.
A program may use at most 128 MiB of HBM per device.

v0:
```python
import math
import jax
import jax.numpy as jnp
from jax import lax
from jax.sharding import PartitionSpec as P

SWEEPS = 4
STEPS = 6
SENS_DEV = 160
advect_speed = 0.3


def with_halo(value, sides, width):
    for axis, dim in sides:
        size, length = (lax.axis_size(axis), value.shape[dim])
        up = [(i, (i + 1) % size) for i in range(size)]
        down = [(j, i) for i, j in up]
        last = lax.slice_in_dim(value, length - width, length, axis=dim)
        first = lax.slice_in_dim(value, 0, width, axis=dim)
        before = lax.ppermute(last, axis, up)
        after = lax.ppermute(first, axis, down)
        value = jnp.concatenate([before, value, after], axis=dim)
    return value


def neighbours(extended):
    middle = extended[:, :, 1:-1]
    west_cells = extended[:, :, :-2]
    east_cells = extended[:, :, 2:]
    side_pad = jnp.pad(middle, ((0, 0), (0, 0), (0, 0), (1, 1)))
    depth_pad = jnp.pad(middle, ((0, 0), (1, 1), (0, 0), (0, 0)))
    beside_all = (
        west_cells
        + east_cells
        + (side_pad[..., :-2] + side_pad[..., 2:])
        + (depth_pad[:, :-2] + depth_pad[:, 2:])
    )
    return (middle, west_cells, east_cells, beside_all)


def prior_apply(source, diagonal):
    state = source / diagonal
    for sweep in range(SWEEPS):
        extended = with_halo(state, (("field", 2),), 1)
        middle, west_cells, east_cells, beside_all = neighbours(extended)
        state = (source + beside_all) / diagonal
    return state


def on_device(
    probes,
    matern_shift,
    diffusivity,
    sensor_count,
    sensor_cell,
    sensor_owner,
    design_logit,
    noise_precision,
):
    probe_count = probes.shape[0]
    block_cx = probes.shape[2]
    cell_count = probes.shape[1] * probes.shape[2] * probes.shape[3]
    field_count = lax.axis_size("field")
    slot_cap = design_logit.shape[2]
    slot_count = sensor_cell.shape[1]
    diagonal = matern_shift + 6.0
    depth = 2
    coef_wide = with_halo(diffusivity, (("field", 1),), depth)
    state = prior_apply(probes.astype(jnp.float32), diagonal)
    for rounds in range(STEPS // depth):
        extended = with_halo(state, (("field", 2),), depth)
        for inner in range(depth):
            width = block_cx + 2 * (depth - inner - 1)
            coef_mid = coef_wide[:, inner + 1 : inner + 1 + width]
            middle, west_cells, east_cells, beside_all = neighbours(extended)
            extended = (
                middle
                + coef_mid * (beside_all - 6.0 * middle)
                - advect_speed * (middle - west_cells)
            )
        state = extended
    slots = jnp.arange(slot_count, dtype=jnp.int32)
    live = (slots < sensor_count[0]).astype(jnp.float32)
    cells = sensor_cell[0]
    owner = sensor_owner[0, :, 0]
    same = owner[:, None] == owner[None, :]
    earlier = slots[None, :] < slots[:, None]
    position = jnp.sum(jnp.logical_and(same, earlier), axis=1)
    target = owner * slot_cap + position
    table = (
        jnp.arange(field_count * slot_cap, dtype=jnp.int32)[:, None] == target[None, :]
    ).astype(jnp.float32)
    flat_state = state.reshape(probe_count, cell_count)
    observed = jnp.take(flat_state, cells, axis=1) * live[None, :]
    outgoing = lax.dot_general(
        table, observed, (((1,), (1,)), ((), ())), precision=lax.Precision.HIGHEST
    )
    outgoing = outgoing.reshape(field_count, slot_cap, probe_count)
    received = lax.all_to_all(outgoing, "field", split_axis=0, concat_axis=0, tiled=True)
    gated = jax.nn.sigmoid(design_logit[0])
    weight_slot = gated * noise_precision[0]
    weighted = received * weight_slot[:, :, None]
    returned = lax.all_to_all(weighted, "field", split_axis=0, concat_axis=0, tiled=True)
    per_sensor = lax.dot_general(
        table,
        returned.reshape(field_count * slot_cap, probe_count),
        (((0,), (0,)), ((), ())),
        precision=lax.Precision.HIGHEST,
    )
    injected = jnp.zeros((probe_count, cell_count), jnp.float32).at[:, cells].add(per_sensor.T)
    adjoint = injected.reshape(probes.shape)
    for rounds in range(STEPS // depth):
        extended = with_halo(adjoint, (("field", 2),), depth)
        for inner in range(depth):
            width = block_cx + 2 * (depth - inner)
            scaled = coef_wide[:, inner : inner + width] * extended
            scaled_mid, scaled_west, scaled_east, scaled_around = neighbours(scaled)
            middle = extended[:, :, 1:-1]
            east_cells = extended[:, :, 2:]
            extended = (
                middle + (scaled_around - 6.0 * scaled_mid) - advect_speed * (middle - east_cells)
            )
        adjoint = extended
    hessian_probes = prior_apply(adjoint, diagonal)
    flat_result = hessian_probes.reshape(probe_count, cell_count)
    piece = lax.all_gather(probes, "probe", axis=0, tiled=True)
    flat_piece = piece.reshape(piece.shape[0], cell_count).astype(jnp.float32)
    columns = lax.dot_general(
        flat_result, flat_piece, (((1,), (1,)), ((), ())), precision=lax.Precision.HIGHEST
    )
    scale_factor = 1.0 / math.sqrt(SENS_DEV * field_count)
    tiles = lax.psum(columns, "field") * scale_factor
    squares = jnp.sum(received * received, axis=2)
    total_squares = lax.psum(squares, "probe")
    weight_grad = gated * (1.0 - gated) * noise_precision[0] * total_squares
    return (hessian_probes, tiles, weight_grad[None])


def solution(mesh):
    in_specs = (
        P("probe", None, "field", None),
        P(None, "field", None),
        P(None, "field", None),
        P("field"),
        P("field", None),
        P("field", None, None),
        P("field", None, None),
        P("field", None, None),
    )
    out_specs = (P("probe", None, "field", None), P("probe", None), P("field", None, None))
    return jax.shard_map(
        on_device, mesh=mesh, in_specs=in_specs, out_specs=out_specs, check_vma=False
    )
```

profile of v0, /device:TPU:0, one launch (start us, length us, event | category | flops | bytes accessed | tf_op | source)
XLA Modules:
  0.0 235.5 jit_solution(16700310639509512461)
XLA Ops:
  10.0 5.0 %collective-permute-start.1 = (f32[8,4,1,256]{3,2,1,0:T(1,128)S(1)}, f32[8,4,1,256]{3,2,1,0:T(1,128)S(1)}, u32[]{:S(2)}, u32[]{:S(2)}) collective-permute-start(f32[8,4,1,256]{3,2,1,0:T(1,128)S(1)} %get-tuple-element.44), channel_id=1, source_target_pairs={{2,0},{4,2},{6,4},{8,6},{10,8},{12,10},{14,12},{16,14},{18,16},{20... | collective-permute-start | bytes 98312 | tf_op jit(solution)/shard_map/ppermute | solution.py:21
  15.1 4.4 %collective-permute-start.11 = (f32[4,2,256]{2,1,0:T(2,128)S(1)}, f32[4,2,256]{2,1,0:T(2,128)S(1)}, u32[]{:S(2)}, u32[]{:S(2)}) collective-permute-start(f32[4,2,256]{2,1,0:T(2,128)S(1)} %get-tuple-element.46), channel_id=1, source_target_pairs={{2,0},{4,2},{6,4},{8,6},{10,8},{12,10},{14,12},{16,14},{18,16},{20... | collective-permute-start | bytes 24584 | tf_op jit(solution)/shard_map/ppermute | solution.py:21
  20.4 4.4 %collective-permute-start.3 = (f32[8,4,1,256]{3,2,1,0:T(1,128)S(1)}, f32[8,4,1,256]{3,2,1,0:T(1,128)S(1)}, u32[]{:S(2)}, u32[]{:S(2)}) collective-permute-start(f32[8,4,1,256]{3,2,1,0:T(1,128)S(1)} %get-tuple-element.42), channel_id=1, source_target_pairs={{2,0},{4,2},{6,4},{8,6},{10,8},{12,10},{14,12},{16,14},{18,16},{20... | collective-permute-start | bytes 98312 | tf_op jit(solution)/shard_map/ppermute | solution.py:21
  27.2 4.5 %collective-permute-start.5 = (f32[8,4,1,256]{3,2,1,0:T(1,128)S(1)}, f32[8,4,1,256]{3,2,1,0:T(1,128)S(1)}, u32[]{:S(2)}, u32[]{:S(2)}) collective-permute-start(f32[8,4,1,256]{3,2,1,0:T(1,128)S(1)} %get-tuple-element.40), channel_id=1, source_target_pairs={{2,0},{4,2},{6,4},{8,6},{10,8},{12,10},{14,12},{16,14},{18,16},{20... | collective-permute-start | bytes 98312 | tf_op jit(solution)/shard_map/ppermute | solution.py:21
  34.2 4.4 %collective-permute-start.7 = (f32[8,4,1,256]{3,2,1,0:T(1,128)S(1)}, f32[8,4,1,256]{3,2,1,0:T(1,128)S(1)}, u32[]{:S(2)}, u32[]{:S(2)}) collective-permute-start(f32[8,4,1,256]{3,2,1,0:T(1,128)S(1)} %get-tuple-element.38), channel_id=1, source_target_pairs={{2,0},{4,2},{6,4},{8,6},{10,8},{12,10},{14,12},{16,14},{18,16},{20... | collective-permute-start | bytes 98312 | tf_op jit(solution)/shard_map/ppermute | solution.py:21
  38.7 1.7 collective-permute-done.6
  41.2 4.5 %collective-permute-start.9 = (f32[8,4,2,256]{3,2,1,0:T(2,128)S(1)}, f32[8,4,2,256]{3,2,1,0:T(2,128)S(1)}, u32[]{:S(2)}, u32[]{:S(2)}) collective-permute-start(f32[8,4,2,256]{3,2,1,0:T(2,128)S(1)} %get-tuple-element.36), channel_id=1, source_target_pairs={{2,0},{4,2},{6,4},{8,6},{10,8},{12,10},{14,12},{16,14},{18,16},{20... | collective-permute-start | bytes 196616 | tf_op jit(solution)/shard_map/ppermute | solution.py:21
  45.8 1.8 collective-permute-done.8
  49.8 4.5 %collective-permute-start.13 = (f32[8,4,2,256]{3,2,1,0:T(2,128)S(1)}, f32[8,4,2,256]{3,2,1,0:T(2,128)S(1)}, u32[]{:S(2)}, u32[]{:S(2)}) collective-permute-start(f32[8,4,2,256]{3,2,1,0:T(2,128)S(1)} %get-tuple-element.34), channel_id=1, source_target_pairs={{2,0},{4,2},{6,4},{8,6},{10,8},{12,10},{14,12},{16,14},{18,16},{20... | collective-permute-start | bytes 196616 | tf_op jit(solution)/shard_map/ppermute | solution.py:21
  54.3 1.9 collective-permute-done.12
  58.4 4.7 %collective-permute-start.15 = (f32[8,4,2,256]{3,2,1,0:T(2,128)S(1)}, f32[8,4,2,256]{3,2,1,0:T(2,128)S(1)}, u32[]{:S(2)}, u32[]{:S(2)}) collective-permute-start(f32[8,4,2,256]{3,2,1,0:T(2,128)S(1)} %get-tuple-element.32), channel_id=1, source_target_pairs={{2,0},{4,2},{6,4},{8,6},{10,8},{12,10},{14,12},{16,14},{18,16},{20... | collective-permute-start | bytes 196616 | tf_op jit(solution)/shard_map/ppermute | solution.py:21
  63.2 1.7 collective-permute-done.14
  67.1 8.6 %copy.46 = f32[8,4,32,256]{0,3,2,1:T(8,128)} copy(f32[8,4,32,256]{3,2,1,0:T(8,128)S(1)} %fusion.88) | data formatting | bytes 2097152 | tf_op jit(solution)/shard_map/sub | solution.py:77
  75.7 6.5 %gather_fusion = f32[256,8]{1,0:T(8,128)S(1)} fusion(f32[8,32768]{0,1:T(8,128)} %bitcast.35, s32[1024]{0:T(1024)S(1)} %pad_clamp_fusion), kind=kCustom, calls=%fused_computation | custom fusion | bytes 17408 | tf_op jit(solution)/shard_map/jit(_take)/gather | solution.py:94
  83.4 5.9 %all-to-all-start = ((f32[16,1,192]{2,1,0:T(1,128)}), f32[16,1,192]{2,1,0:T(1,128)S(1)}, u32[]{:S(2)}, u32[]{:S(2)}) async-start(f32[16,1,192]{2,1,0:T(1,128)} %reshape.115), calls=%async_computation | async-start | bytes 32768 | tf_op jit(solution)/shard_map/all_to_all | solution.py:99
  89.4 6.4 %all-to-all-done = f32[16,1,192]{2,1,0:T(1,128)S(1)} async-done(((f32[16,1,192]{2,1,0:T(1,128)}), f32[16,1,192]{2,1,0:T(1,128)S(1)}, u32[]{:S(2)}, u32[]{:S(2)}) %all-to-all-start) | async-done | bytes 12320 | tf_op jit(solution)/shard_map/all_to_all | solution.py:99
  97.2 9.1 %all_to_all.10 = f32[16,1,192]{2,1,0:T(1,128)S(1)} all-to-all(f32[16,1,192]{2,1,0:T(1,128)S(1)} %reshape.117), channel_id=1, replica_groups=mesh['field'=16,'probe'=2] {'field'}, dimensions={0} | all-to-all | bytes 24576 | tf_op jit(solution)/shard_map/all_to_all | solution.py:103
  107.6 8.2 %scatter_custom_fusion = f32[8,32768]{0,1:T(8,128)} fusion(s32[256]{0:T(256)S(1)} %bitcast.43, f32[256,8]{1,0:T(8,128)S(1)} %fusion.154, f32[]{:T(128)} %constant.10.clone.1), kind=kCustom, calls=%fused_computation.2 | custom fusion | flops 2048 | bytes 1048580 | tf_op jit(solution)/shard_map/scatter-add | solution.py:110
  115.8 9.8 %copy.50 = f32[8,4,32,256]{3,2,1,0:T(8,128)S(1)} copy(f32[8,4,32,256]{0,3,2,1:T(8,128)} %bitcast.34) | data formatting | bytes 2097152 | tf_op jit(solution)/shard_map/reshape | solution.py:111
  125.8 4.4 %collective-permute-start.17 = (f32[8,4,2,256]{3,2,1,0:T(2,128)S(1)}, f32[8,4,2,256]{3,2,1,0:T(2,128)S(1)}, u32[]{:S(2)}, u32[]{:S(2)}) collective-permute-start(f32[8,4,2,256]{3,2,1,0:T(2,128)S(1)} %get-tuple-element.30), channel_id=1, source_target_pairs={{2,0},{4,2},{6,4},{8,6},{10,8},{12,10},{14,12},{16,14},{18,16},{20... | collective-permute-start | bytes 196616 | tf_op jit(solution)/shard_map/ppermute | solution.py:21
  130.2 1.9 collective-permute-done.16
  134.9 4.7 %collective-permute-start.19 = (f32[8,4,2,256]{3,2,1,0:T(2,128)S(1)}, f32[8,4,2,256]{3,2,1,0:T(2,128)S(1)}, u32[]{:S(2)}, u32[]{:S(2)}) collective-permute-start(f32[8,4,2,256]{3,2,1,0:T(2,128)S(1)} %get-tuple-element.28), channel_id=1, source_target_pairs={{2,0},{4,2},{6,4},{8,6},{10,8},{12,10},{14,12},{16,14},{18,16},{20... | collective-permute-start | bytes 196616 | tf_op jit(solution)/shard_map/ppermute | solution.py:21
  144.2 4.5 %collective-permute-start.21 = (f32[8,4,2,256]{3,2,1,0:T(2,128)S(1)}, f32[8,4,2,256]{3,2,1,0:T(2,128)S(1)}, u32[]{:S(2)}, u32[]{:S(2)}) collective-permute-start(f32[8,4,2,256]{3,2,1,0:T(2,128)S(1)} %get-tuple-element.26), channel_id=1, source_target_pairs={{2,0},{4,2},{6,4},{8,6},{10,8},{12,10},{14,12},{16,14},{18,16},{20... | collective-permute-start | bytes 196616 | tf_op jit(solution)/shard_map/ppermute | solution.py:21
  148.7 1.9 collective-permute-done.20
  153.4 4.5 %collective-permute-start.23 = (f32[8,4,1,256]{3,2,1,0:T(1,128)S(1)}, f32[8,4,1,256]{3,2,1,0:T(1,128)S(1)}, u32[]{:S(2)}, u32[]{:S(2)}) collective-permute-start(f32[8,4,1,256]{3,2,1,0:T(1,128)S(1)} %get-tuple-element.24), channel_id=1, source_target_pairs={{2,0},{4,2},{6,4},{8,6},{10,8},{12,10},{14,12},{16,14},{18,16},{20... | collective-permute-start | bytes 98312 | tf_op jit(solution)/shard_map/ppermute | solution.py:21
  160.4 4.6 %collective-permute-start.25 = (f32[8,4,1,256]{3,2,1,0:T(1,128)S(1)}, f32[8,4,1,256]{3,2,1,0:T(1,128)S(1)}, u32[]{:S(2)}, u32[]{:S(2)}) collective-permute-start(f32[8,4,1,256]{3,2,1,0:T(1,128)S(1)} %get-tuple-element.22), channel_id=1, source_target_pairs={{2,0},{4,2},{6,4},{8,6},{10,8},{12,10},{14,12},{16,14},{18,16},{20... | collective-permute-start | bytes 98312 | tf_op jit(solution)/shard_map/ppermute | solution.py:21
  167.4 4.5 %collective-permute-start.27 = (f32[8,4,1,256]{3,2,1,0:T(1,128)S(1)}, f32[8,4,1,256]{3,2,1,0:T(1,128)S(1)}, u32[]{:S(2)}, u32[]{:S(2)}) collective-permute-start(f32[8,4,1,256]{3,2,1,0:T(1,128)S(1)} %get-tuple-element.20), channel_id=1, source_target_pairs={{2,0},{4,2},{6,4},{8,6},{10,8},{12,10},{14,12},{16,14},{18,16},{20... | collective-permute-start | bytes 98312 | tf_op jit(solution)/shard_map/ppermute | solution.py:21
  173.0 5.0 %psum.15 = f32[16,24]{1,0:T(8,128)S(1)} all-reduce(f32[16,24]{1,0:T(8,128)S(1)} %get-tuple-element.47), channel_id=1, replica_groups=mesh['field'=16,'probe'=2] {'probe'}, use_global_device_ids=true, to_apply=%region_4.5 | all-reduce | flops 384 | bytes 3072 | tf_op jit(solution)/shard_map/psum | solution.py:134
  178.8 4.4 %collective-permute-start.29 = (f32[8,4,1,256]{3,2,1,0:T(1,128)S(1)}, f32[8,4,1,256]{3,2,1,0:T(1,128)S(1)}, u32[]{:S(2)}, u32[]{:S(2)}) collective-permute-start(f32[8,4,1,256]{3,2,1,0:T(1,128)S(1)} %get-tuple-element.18), channel_id=1, source_target_pairs={{2,0},{4,2},{6,4},{8,6},{10,8},{12,10},{14,12},{16,14},{18,16},{20... | collective-permute-start | bytes 98312 | tf_op jit(solution)/shard_map/ppermute | solution.py:21
  185.6 6.6 %all-gather.2.cloned.1.call-done = bf16[16,4,32,256]{3,0,2,1:T(8,128)(2,1)} async-done(((bf16[8,4,32,256]{3,0,2,1:T(8,128)(2,1)}), bf16[16,4,32,256]{3,0,2,1:T(8,128)(2,1)}) %all-gather.2.cloned.1.call-update) | async-done | bytes 1048592 | tf_op jit(solution)/shard_map/all_gather | solution.py:126
  192.1 2.9 %convolution_bitcast_fusion = f32[8,16]{1,0:T(8,128)S(1)} fusion(bf16[16,4,32,256]{3,0,2,1:T(8,128)(2,1)} %all-gather.2.cloned.1.call-done, f32[8,4,32,256]{3,2,1,0:T(8,128)S(1)} %fusion.133), kind=kOutput, calls=%fused_computation.158 | convolution fusion | flops 50331648 | bytes 2097664 | tf_op jit(solution)/shard_map/dot_general | solution.py:128
  195.0 33.0 %psum.14 = f32[8,16]{1,0:T(8,128)S(1)} all-reduce(f32[8,16]{1,0:T(8,128)S(1)} %convolution_bitcast_fusion), channel_id=1, replica_groups=mesh['field'=16,'probe'=2] {'field'}, use_global_device_ids=true, to_apply=%region_2.3 | all-reduce | flops 128 | bytes 1024 | tf_op jit(solution)/shard_map/psum | solution.py:132
  (132 shorter events, 39.1 us)
Async XLA Ops:
  9.4 10.1 %collective-permute-start = (f32[8,4,1,256]{3,2,1,0:T(1,128)S(1)}, f32[8,4,1,256]{3,2,1,0:T(1,128)S(1)}, u32[]{:S(2)}, u32[]{:S(2)}) collective-permute-start(f32[8,4,1,256]{3,2,1,0:T(1,128)S(1)} %get-tuple-element.43), channel_id=1, source_target_pairs={{0,2},{2,4},{4,6},{6,8},{8,10},{10,12},{12,14},{14,16},{16,18},{18... | collective-permute-start | bytes 98312 | tf_op jit(solution)/shard_map/ppermute | solution.py:20
  10.0 9.6 %collective-permute-start.1 = (f32[8,4,1,256]{3,2,1,0:T(1,128)S(1)}, f32[8,4,1,256]{3,2,1,0:T(1,128)S(1)}, u32[]{:S(2)}, u32[]{:S(2)}) collective-permute-start(f32[8,4,1,256]{3,2,1,0:T(1,128)S(1)} %get-tuple-element.44), channel_id=1, source_target_pairs={{2,0},{4,2},{6,4},{8,6},{10,8},{12,10},{14,12},{16,14},{18,16},{20... | collective-permute-start | bytes 98312 | tf_op jit(solution)/shard_map/ppermute | solution.py:21
  15.0 30.7 %collective-permute-start.10 = (f32[4,2,256]{2,1,0:T(2,128)S(1)}, f32[4,2,256]{2,1,0:T(2,128)S(1)}, u32[]{:S(2)}, u32[]{:S(2)}) collective-permute-start(f32[4,2,256]{2,1,0:T(2,128)S(1)} %get-tuple-element.45), channel_id=1, source_target_pairs={{0,2},{2,4},{4,6},{6,8},{8,10},{10,12},{12,14},{14,16},{16,18},{18... | collective-permute-start | bytes 24584 | tf_op jit(solution)/shard_map/ppermute | solution.py:20
  15.1 30.6 %collective-permute-start.11 = (f32[4,2,256]{2,1,0:T(2,128)S(1)}, f32[4,2,256]{2,1,0:T(2,128)S(1)}, u32[]{:S(2)}, u32[]{:S(2)}) collective-permute-start(f32[4,2,256]{2,1,0:T(2,128)S(1)} %get-tuple-element.46), channel_id=1, source_target_pairs={{2,0},{4,2},{6,4},{8,6},{10,8},{12,10},{14,12},{16,14},{18,16},{20... | collective-permute-start | bytes 24584 | tf_op jit(solution)/shard_map/ppermute | solution.py:21
  20.3 6.1 %collective-permute-start.2 = (f32[8,4,1,256]{3,2,1,0:T(1,128)S(1)}, f32[8,4,1,256]{3,2,1,0:T(1,128)S(1)}, u32[]{:S(2)}, u32[]{:S(2)}) collective-permute-start(f32[8,4,1,256]{3,2,1,0:T(1,128)S(1)} %get-tuple-element.41), channel_id=1, source_target_pairs={{0,2},{2,4},{4,6},{6,8},{8,10},{10,12},{12,14},{14,16},{16,18},{18... | collective-permute-start | bytes 98312 | tf_op jit(solution)/shard_map/ppermute | solution.py:20
  20.4 6.0 %collective-permute-start.3 = (f32[8,4,1,256]{3,2,1,0:T(1,128)S(1)}, f32[8,4,1,256]{3,2,1,0:T(1,128)S(1)}, u32[]{:S(2)}, u32[]{:S(2)}) collective-permute-start(f32[8,4,1,256]{3,2,1,0:T(1,128)S(1)} %get-tuple-element.42), channel_id=1, source_target_pairs={{2,0},{4,2},{6,4},{8,6},{10,8},{12,10},{14,12},{16,14},{18,16},{20... | collective-permute-start | bytes 98312 | tf_op jit(solution)/shard_map/ppermute | solution.py:21
  27.2 6.2 %collective-permute-start.4 = (f32[8,4,1,256]{3,2,1,0:T(1,128)S(1)}, f32[8,4,1,256]{3,2,1,0:T(1,128)S(1)}, u32[]{:S(2)}, u32[]{:S(2)}) collective-permute-start(f32[8,4,1,256]{3,2,1,0:T(1,128)S(1)} %get-tuple-element.39), channel_id=1, source_target_pairs={{0,2},{2,4},{4,6},{6,8},{8,10},{10,12},{12,14},{14,16},{16,18},{18... | collective-permute-start | bytes 98312 | tf_op jit(solution)/shard_map/ppermute | solution.py:20
  27.2 6.1 %collective-permute-start.5 = (f32[8,4,1,256]{3,2,1,0:T(1,128)S(1)}, f32[8,4,1,256]{3,2,1,0:T(1,128)S(1)}, u32[]{:S(2)}, u32[]{:S(2)}) collective-permute-start(f32[8,4,1,256]{3,2,1,0:T(1,128)S(1)} %get-tuple-element.40), channel_id=1, source_target_pairs={{2,0},{4,2},{6,4},{8,6},{10,8},{12,10},{14,12},{16,14},{18,16},{20... | collective-permute-start | bytes 98312 | tf_op jit(solution)/shard_map/ppermute | solution.py:21
  34.2 6.2 %collective-permute-start.6 = (f32[8,4,1,256]{3,2,1,0:T(1,128)S(1)}, f32[8,4,1,256]{3,2,1,0:T(1,128)S(1)}, u32[]{:S(2)}, u32[]{:S(2)}) collective-permute-start(f32[8,4,1,256]{3,2,1,0:T(1,128)S(1)} %get-tuple-element.37), channel_id=1, source_target_pairs={{0,2},{2,4},{4,6},{6,8},{8,10},{10,12},{12,14},{14,16},{16,18},{18... | collective-permute-start | bytes 98312 | tf_op jit(solution)/shard_map/ppermute | solution.py:20
  34.2 6.1 %collective-permute-start.7 = (f32[8,4,1,256]{3,2,1,0:T(1,128)S(1)}, f32[8,4,1,256]{3,2,1,0:T(1,128)S(1)}, u32[]{:S(2)}, u32[]{:S(2)}) collective-permute-start(f32[8,4,1,256]{3,2,1,0:T(1,128)S(1)} %get-tuple-element.38), channel_id=1, source_target_pairs={{2,0},{4,2},{6,4},{8,6},{10,8},{12,10},{14,12},{16,14},{18,16},{20... | collective-permute-start | bytes 98312 | tf_op jit(solution)/shard_map/ppermute | solution.py:21
  41.1 6.5 %collective-permute-start.8 = (f32[8,4,2,256]{3,2,1,0:T(2,128)S(1)}, f32[8,4,2,256]{3,2,1,0:T(2,128)S(1)}, u32[]{:S(2)}, u32[]{:S(2)}) collective-permute-start(f32[8,4,2,256]{3,2,1,0:T(2,128)S(1)} %get-tuple-element.35), channel_id=1, source_target_pairs={{0,2},{2,4},{4,6},{6,8},{8,10},{10,12},{12,14},{14,16},{16,18},{18... | collective-permute-start | bytes 196616 | tf_op jit(solution)/shard_map/ppermute | solution.py:20
  41.2 6.4 %collective-permute-start.9 = (f32[8,4,2,256]{3,2,1,0:T(2,128)S(1)}, f32[8,4,2,256]{3,2,1,0:T(2,128)S(1)}, u32[]{:S(2)}, u32[]{:S(2)}) collective-permute-start(f32[8,4,2,256]{3,2,1,0:T(2,128)S(1)} %get-tuple-element.36), channel_id=1, source_target_pairs={{2,0},{4,2},{6,4},{8,6},{10,8},{12,10},{14,12},{16,14},{18,16},{20... | collective-permute-start | bytes 196616 | tf_op jit(solution)/shard_map/ppermute | solution.py:21
  49.7 6.5 %collective-permute-start.12 = (f32[8,4,2,256]{3,2,1,0:T(2,128)S(1)}, f32[8,4,2,256]{3,2,1,0:T(2,128)S(1)}, u32[]{:S(2)}, u32[]{:S(2)}) collective-permute-start(f32[8,4,2,256]{3,2,1,0:T(2,128)S(1)} %get-tuple-element.33), channel_id=1, source_target_pairs={{0,2},{2,4},{4,6},{6,8},{8,10},{10,12},{12,14},{14,16},{16,18},{18... | collective-permute-start | bytes 196616 | tf_op jit(solution)/shard_map/ppermute | solution.py:20
  49.8 6.4 %collective-permute-start.13 = (f32[8,4,2,256]{3,2,1,0:T(2,128)S(1)}, f32[8,4,2,256]{3,2,1,0:T(2,128)S(1)}, u32[]{:S(2)}, u32[]{:S(2)}) collective-permute-start(f32[8,4,2,256]{3,2,1,0:T(2,128)S(1)} %get-tuple-element.34), channel_id=1, source_target_pairs={{2,0},{4,2},{6,4},{8,6},{10,8},{12,10},{14,12},{16,14},{18,16},{20... | collective-permute-start | bytes 196616 | tf_op jit(solution)/shard_map/ppermute | solution.py:21
  58.4 6.5 %collective-permute-start.14 = (f32[8,4,2,256]{3,2,1,0:T(2,128)S(1)}, f32[8,4,2,256]{3,2,1,0:T(2,128)S(1)}, u32[]{:S(2)}, u32[]{:S(2)}) collective-permute-start(f32[8,4,2,256]{3,2,1,0:T(2,128)S(1)} %get-tuple-element.31), channel_id=1, source_target_pairs={{0,2},{2,4},{4,6},{6,8},{8,10},{10,12},{12,14},{14,16},{16,18},{18... | collective-permute-start | bytes 196616 | tf_op jit(solution)/shard_map/ppermute | solution.py:20
  58.4 6.6 %collective-permute-start.15 = (f32[8,4,2,256]{3,2,1,0:T(2,128)S(1)}, f32[8,4,2,256]{3,2,1,0:T(2,128)S(1)}, u32[]{:S(2)}, u32[]{:S(2)}) collective-permute-start(f32[8,4,2,256]{3,2,1,0:T(2,128)S(1)} %get-tuple-element.32), channel_id=1, source_target_pairs={{2,0},{4,2},{6,4},{8,6},{10,8},{12,10},{14,12},{16,14},{18,16},{20... | collective-permute-start | bytes 196616 | tf_op jit(solution)/shard_map/ppermute | solution.py:21
  83.4 12.4 %all-to-all-start = ((f32[16,1,192]{2,1,0:T(1,128)}), f32[16,1,192]{2,1,0:T(1,128)S(1)}, u32[]{:S(2)}, u32[]{:S(2)}) async-start(f32[16,1,192]{2,1,0:T(1,128)} %reshape.115), calls=%async_computation | async-start | bytes 32768 | tf_op jit(solution)/shard_map/all_to_all | solution.py:99
  89.3 102.8 %all-gather.2.cloned.1.call-start = ((), (), s32[]{:S(2)}) async-start(), calls=%async_computation.2 | async-start | bytes 1572864 | tf_op jit(solution)/shard_map/all_gather | solution.py:126
  125.7 6.4 %collective-permute-start.16 = (f32[8,4,2,256]{3,2,1,0:T(2,128)S(1)}, f32[8,4,2,256]{3,2,1,0:T(2,128)S(1)}, u32[]{:S(2)}, u32[]{:S(2)}) collective-permute-start(f32[8,4,2,256]{3,2,1,0:T(2,128)S(1)} %get-tuple-element.29), channel_id=1, source_target_pairs={{0,2},{2,4},{4,6},{6,8},{8,10},{10,12},{12,14},{14,16},{16,18},{18... | collective-permute-start | bytes 196616 | tf_op jit(solution)/shard_map/ppermute | solution.py:20
  125.8 6.4 %collective-permute-start.17 = (f32[8,4,2,256]{3,2,1,0:T(2,128)S(1)}, f32[8,4,2,256]{3,2,1,0:T(2,128)S(1)}, u32[]{:S(2)}, u32[]{:S(2)}) collective-permute-start(f32[8,4,2,256]{3,2,1,0:T(2,128)S(1)} %get-tuple-element.30), channel_id=1, source_target_pairs={{2,0},{4,2},{6,4},{8,6},{10,8},{12,10},{14,12},{16,14},{18,16},{20... | collective-permute-start | bytes 196616 | tf_op jit(solution)/shard_map/ppermute | solution.py:21
  134.8 6.4 %collective-permute-start.18 = (f32[8,4,2,256]{3,2,1,0:T(2,128)S(1)}, f32[8,4,2,256]{3,2,1,0:T(2,128)S(1)}, u32[]{:S(2)}, u32[]{:S(2)}) collective-permute-start(f32[8,4,2,256]{3,2,1,0:T(2,128)S(1)} %get-tuple-element.27), channel_id=1, source_target_pairs={{0,2},{2,4},{4,6},{6,8},{8,10},{10,12},{12,14},{14,16},{16,18},{18... | collective-permute-start | bytes 196616 | tf_op jit(solution)/shard_map/ppermute | solution.py:20
  134.9 6.6 %collective-permute-start.19 = (f32[8,4,2,256]{3,2,1,0:T(2,128)S(1)}, f32[8,4,2,256]{3,2,1,0:T(2,128)S(1)}, u32[]{:S(2)}, u32[]{:S(2)}) collective-permute-start(f32[8,4,2,256]{3,2,1,0:T(2,128)S(1)} %get-tuple-element.28), channel_id=1, source_target_pairs={{2,0},{4,2},{6,4},{8,6},{10,8},{12,10},{14,12},{16,14},{18,16},{20... | collective-permute-start | bytes 196616 | tf_op jit(solution)/shard_map/ppermute | solution.py:21
  144.1 6.5 %collective-permute-start.20 = (f32[8,4,2,256]{3,2,1,0:T(2,128)S(1)}, f32[8,4,2,256]{3,2,1,0:T(2,128)S(1)}, u32[]{:S(2)}, u32[]{:S(2)}) collective-permute-start(f32[8,4,2,256]{3,2,1,0:T(2,128)S(1)} %get-tuple-element.25), channel_id=1, source_target_pairs={{0,2},{2,4},{4,6},{6,8},{8,10},{10,12},{12,14},{14,16},{16,18},{18... | collective-permute-start | bytes 196616 | tf_op jit(solution)/shard_map/ppermute | solution.py:20
  144.2 6.4 %collective-permute-start.21 = (f32[8,4,2,256]{3,2,1,0:T(2,128)S(1)}, f32[8,4,2,256]{3,2,1,0:T(2,128)S(1)}, u32[]{:S(2)}, u32[]{:S(2)}) collective-permute-start(f32[8,4,2,256]{3,2,1,0:T(2,128)S(1)} %get-tuple-element.26), channel_id=1, source_target_pairs={{2,0},{4,2},{6,4},{8,6},{10,8},{12,10},{14,12},{16,14},{18,16},{20... | collective-permute-start | bytes 196616 | tf_op jit(solution)/shard_map/ppermute | solution.py:21
  153.3 6.2 %collective-permute-start.22 = (f32[8,4,1,256]{3,2,1,0:T(1,128)S(1)}, f32[8,4,1,256]{3,2,1,0:T(1,128)S(1)}, u32[]{:S(2)}, u32[]{:S(2)}) collective-permute-start(f32[8,4,1,256]{3,2,1,0:T(1,128)S(1)} %get-tuple-element.23), channel_id=1, source_target_pairs={{0,2},{2,4},{4,6},{6,8},{8,10},{10,12},{12,14},{14,16},{16,18},{18... | collective-permute-start | bytes 98312 | tf_op jit(solution)/shard_map/ppermute | solution.py:20
  153.4 6.2 %collective-permute-start.23 = (f32[8,4,1,256]{3,2,1,0:T(1,128)S(1)}, f32[8,4,1,256]{3,2,1,0:T(1,128)S(1)}, u32[]{:S(2)}, u32[]{:S(2)}) collective-permute-start(f32[8,4,1,256]{3,2,1,0:T(1,128)S(1)} %get-tuple-element.24), channel_id=1, source_target_pairs={{2,0},{4,2},{6,4},{8,6},{10,8},{12,10},{14,12},{16,14},{18,16},{20... | collective-permute-start | bytes 98312 | tf_op jit(solution)/shard_map/ppermute | solution.py:21
  160.3 6.2 %collective-permute-start.24 = (f32[8,4,1,256]{3,2,1,0:T(1,128)S(1)}, f32[8,4,1,256]{3,2,1,0:T(1,128)S(1)}, u32[]{:S(2)}, u32[]{:S(2)}) collective-permute-start(f32[8,4,1,256]{3,2,1,0:T(1,128)S(1)} %get-tuple-element.21), channel_id=1, source_target_pairs={{0,2},{2,4},{4,6},{6,8},{8,10},{10,12},{12,14},{14,16},{16,18},{18... | collective-permute-start | bytes 98312 | tf_op jit(solution)/shard_map/ppermute | solution.py:20
  160.4 6.2 %collective-permute-start.25 = (f32[8,4,1,256]{3,2,1,0:T(1,128)S(1)}, f32[8,4,1,256]{3,2,1,0:T(1,128)S(1)}, u32[]{:S(2)}, u32[]{:S(2)}) collective-permute-start(f32[8,4,1,256]{3,2,1,0:T(1,128)S(1)} %get-tuple-element.22), channel_id=1, source_target_pairs={{2,0},{4,2},{6,4},{8,6},{10,8},{12,10},{14,12},{16,14},{18,16},{20... | collective-permute-start | bytes 98312 | tf_op jit(solution)/shard_map/ppermute | solution.py:21
  167.4 10.7 %collective-permute-start.26 = (f32[8,4,1,256]{3,2,1,0:T(1,128)S(1)}, f32[8,4,1,256]{3,2,1,0:T(1,128)S(1)}, u32[]{:S(2)}, u32[]{:S(2)}) collective-permute-start(f32[8,4,1,256]{3,2,1,0:T(1,128)S(1)} %get-tuple-element.19), channel_id=1, source_target_pairs={{0,2},{2,4},{4,6},{6,8},{8,10},{10,12},{12,14},{14,16},{16,18},{18... | collective-permute-start | bytes 98312 | tf_op jit(solution)/shard_map/ppermute | solution.py:20
  167.4 10.6 %collective-permute-start.27 = (f32[8,4,1,256]{3,2,1,0:T(1,128)S(1)}, f32[8,4,1,256]{3,2,1,0:T(1,128)S(1)}, u32[]{:S(2)}, u32[]{:S(2)}) collective-permute-start(f32[8,4,1,256]{3,2,1,0:T(1,128)S(1)} %get-tuple-element.20), channel_id=1, source_target_pairs={{2,0},{4,2},{6,4},{8,6},{10,8},{12,10},{14,12},{16,14},{18,16},{20... | collective-permute-start | bytes 98312 | tf_op jit(solution)/shard_map/ppermute | solution.py:21
  178.8 6.1 %collective-permute-start.28 = (f32[8,4,1,256]{3,2,1,0:T(1,128)S(1)}, f32[8,4,1,256]{3,2,1,0:T(1,128)S(1)}, u32[]{:S(2)}, u32[]{:S(2)}) collective-permute-start(f32[8,4,1,256]{3,2,1,0:T(1,128)S(1)} %get-tuple-element.17), channel_id=1, source_target_pairs={{0,2},{2,4},{4,6},{6,8},{8,10},{10,12},{12,14},{14,16},{16,18},{18... | collective-permute-start | bytes 98312 | tf_op jit(solution)/shard_map/ppermute | solution.py:20
  178.8 6.0 %collective-permute-start.29 = (f32[8,4,1,256]{3,2,1,0:T(1,128)S(1)}, f32[8,4,1,256]{3,2,1,0:T(1,128)S(1)}, u32[]{:S(2)}, u32[]{:S(2)}) collective-permute-start(f32[8,4,1,256]{3,2,1,0:T(1,128)S(1)} %get-tuple-element.18), channel_id=1, source_target_pairs={{2,0},{4,2},{6,4},{8,6},{10,8},{12,10},{14,12},{16,14},{18,16},{20... | collective-permute-start | bytes 98312 | tf_op jit(solution)/shard_map/ppermute | solution.py:21
  (7 other events, 123.8 us)
Sparse Core Ops, SparseCore 0:
  173.1 18.9 all-gather.1
where the time goes:
time: 236 us
  starting transfers between devices  75.5 us (32%)
  blocking collectives  47.1 us (20%)
  waiting for transfers between devices  32.7 us (14%)
  other arithmetic  31.7 us (13%)
  local copies, waits for them, and re-layouts  29.5 us (12%)
  between operations  15.3 us (6%)
  matrix products  3.61 us (2%)
    ppermute x15, starting transfers between devices, with_halo(): after = lax.ppermute(first, axis, down)  68.3 us
    psum x1, blocking collectives, on_device(): tiles = lax.psum(columns, 'field') * scale_factor  33 us
    ppermute x15, waiting for transfers between devices, with_halo(): before = lax.ppermute(last, axis, up)  19.2 us
    reshape x1, local copies, waits for them, and re-layouts, on_device(): adjoint = injected.reshape(probes.shape)  9.83 us
    all_to_all x1, blocking collectives, on_device(): lax.all_to_all(weighted, 'field', split_axis=0, concat_axis=0, tiled=True)  9.07 us
    sub x1, local copies, waits for them, and re-layouts, on_device(): middle + coef_mid * (beside_all - 6.0 * middle)  8.58 us
    scatter-add x1, other arithmetic, on_device(): jnp.zeros((probe_count, cell_count), jnp.float32).at[:, cells]  8.2 us
    all_gather x1, waiting for transfers between devices, on_device(): piece = lax.all_gather(probes, 'probe', axis=0, tiled=True)  6.56 us
  transfers between devices with their start and end apart: 32, of which 16 were waited for; matrix products, arithmetic and copies ran while one was open for 3% of the time, Pallas kernels for 0%

commit v1 on v0

--- a/solution.py
+++ b/solution.py
@@ -8,6 +8,28 @@
 STEPS = 6
 SENS_DEV = 160
 advect_speed = 0.3
+
+
+def in_order(pieces, dim):
+    lengths = list(pieces.shape[1:])
+    lengths[dim] *= pieces.shape[0]
+    return jnp.moveaxis(pieces, 0, dim).reshape(lengths)
+
+
+def doubled(x, axis):
+    size = lax.axis_size(axis)
+    pieces = x[None]
+    for level in range(size.bit_length() - 1):
+        bit = 1 << level
+        other = lax.ppermute(pieces, axis, [(i, i ^ bit) for i in range(size)])
+        both = jnp.stack([pieces, other])
+        upper = lax.axis_index(axis) >> level & 1
+        pieces = jnp.where(upper == 0, both, both[::-1]).reshape(-1, *x.shape)
+    return pieces
+
+
+def doubled_up(array, axis, dim):
+    return in_order(doubled(array, axis), dim)
 
 
 def with_halo(value, sides, width):
@@ -123,7 +145,7 @@
         adjoint = extended
     hessian_probes = prior_apply(adjoint, diagonal)
     flat_result = hessian_probes.reshape(probe_count, cell_count)
-    piece = lax.all_gather(probes, "probe", axis=0, tiled=True)
+    piece = doubled_up(probes, "probe", 0)
     flat_piece = piece.reshape(piece.shape[0], cell_count).astype(jnp.float32)
     columns = lax.dot_general(
         flat_result, flat_piece, (((1,), (1,)), ((), ())), precision=lax.Precision.HIGHEST

time: 236 us -> 221 us (0.936)
  between operations: 15.3 us -> 1.97 us
  waiting for transfers between devices: 32.7 us -> 24.6 us
  local copies, waits for them, and re-layouts: 29.5 us -> 32.4 us
    all_gather x1 -> x0, waiting for transfers between devices: 6.56 us -> none  [on_device(): piece = lax.all_gather(probes, 'probe', axis=0, tiled=True)]
    psum x1, blocking collectives: 5 us -> 8.3 us  [on_device(): total_squares = lax.psum(squares, 'probe')]
  transfers between devices with their start and end apart: 32 -> 32, of which waited for: 16 -> 13; matrix products, arithmetic and copies ran while one was open for 3% -> 4% of each run, Pallas kernels for 0% -> 0%
where the time goes in v1:
time: 221 us
  starting transfers between devices  77.3 us (35%)
  blocking collectives  49.3 us (22%)
  other arithmetic  33.1 us (15%)
  local copies, waits for them, and re-layouts  32.4 us (15%)
  waiting for transfers between devices  24.6 us (11%)
    ppermute x15, starting transfers between devices, with_halo(): after = lax.ppermute(first, axis, down)  67.9 us
    psum x1, blocking collectives, on_device(): tiles = lax.psum(columns, 'field') * scale_factor  31.9 us
    ppermute x15, waiting for transfers between devices, with_halo(): before = lax.ppermute(last, axis, up)  17.8 us
    reshape x1, local copies, waits for them, and re-layouts, on_device(): adjoint = injected.reshape(probes.shape)  9.83 us
    all_to_all x1, blocking collectives, on_device(): lax.all_to_all(weighted, 'field', split_axis=0, concat_axis=0, tiled=True)  9.07 us
    sub x1, local copies, waits for them, and re-layouts, on_device(): middle + coef_mid * (beside_all - 6.0 * middle)  8.58 us
    psum x1, blocking collectives, on_device(): total_squares = lax.psum(squares, 'probe')  8.3 us
    scatter-add x1, other arithmetic, on_device(): jnp.zeros((probe_count, cell_count), jnp.float32).at[:, cells]  8.21 us
  transfers between devices with their start and end apart: 32, of which 13 were waited for; matrix products, arithmetic and copies ran while one was open for 4% of the time, Pallas kernels for 0%

profile of v1, /device:TPU:0, one launch (start us, length us, event | category | flops | bytes accessed | tf_op | source)
XLA Modules:
  0.0 220.6 jit_solution(10343671269348558344)
XLA Ops:
  3.4 5.0 %collective-permute-start.1 = (f32[8,4,1,256]{3,2,1,0:T(1,128)S(1)}, f32[8,4,1,256]{3,2,1,0:T(1,128)S(1)}, u32[]{:S(2)}, u32[]{:S(2)}) collective-permute-start(f32[8,4,1,256]{3,2,1,0:T(1,128)S(1)} %get-tuple-element.44), channel_id=1, source_target_pairs={{2,0},{4,2},{6,4},{8,6},{10,8},{12,10},{14,12},{16,14},{18,16},{20... | collective-permute-start | bytes 98312 | tf_op jit(solution)/shard_map/ppermute | solution.py:43
  8.6 4.4 %collective-permute-start.11 = (f32[4,2,256]{2,1,0:T(2,128)S(1)}, f32[4,2,256]{2,1,0:T(2,128)S(1)}, u32[]{:S(2)}, u32[]{:S(2)}) collective-permute-start(f32[4,2,256]{2,1,0:T(2,128)S(1)} %get-tuple-element.46), channel_id=1, source_target_pairs={{2,0},{4,2},{6,4},{8,6},{10,8},{12,10},{14,12},{16,14},{18,16},{20... | collective-permute-start | bytes 24584 | tf_op jit(solution)/shard_map/ppermute | solution.py:43
  13.8 4.4 %collective-permute-start.3 = (f32[8,4,1,256]{3,2,1,0:T(1,128)S(1)}, f32[8,4,1,256]{3,2,1,0:T(1,128)S(1)}, u32[]{:S(2)}, u32[]{:S(2)}) collective-permute-start(f32[8,4,1,256]{3,2,1,0:T(1,128)S(1)} %get-tuple-element.42), channel_id=1, source_target_pairs={{2,0},{4,2},{6,4},{8,6},{10,8},{12,10},{14,12},{16,14},{18,16},{20... | collective-permute-start | bytes 98312 | tf_op jit(solution)/shard_map/ppermute | solution.py:43
  20.7 4.5 %collective-permute-start.5 = (f32[8,4,1,256]{3,2,1,0:T(1,128)S(1)}, f32[8,4,1,256]{3,2,1,0:T(1,128)S(1)}, u32[]{:S(2)}, u32[]{:S(2)}) collective-permute-start(f32[8,4,1,256]{3,2,1,0:T(1,128)S(1)} %get-tuple-element.40), channel_id=1, source_target_pairs={{2,0},{4,2},{6,4},{8,6},{10,8},{12,10},{14,12},{16,14},{18,16},{20... | collective-permute-start | bytes 98312 | tf_op jit(solution)/shard_map/ppermute | solution.py:43
  27.7 4.4 %collective-permute-start.7 = (f32[8,4,1,256]{3,2,1,0:T(1,128)S(1)}, f32[8,4,1,256]{3,2,1,0:T(1,128)S(1)}, u32[]{:S(2)}, u32[]{:S(2)}) collective-permute-start(f32[8,4,1,256]{3,2,1,0:T(1,128)S(1)} %get-tuple-element.38), channel_id=1, source_target_pairs={{2,0},{4,2},{6,4},{8,6},{10,8},{12,10},{14,12},{16,14},{18,16},{20... | collective-permute-start | bytes 98312 | tf_op jit(solution)/shard_map/ppermute | solution.py:43
  34.7 4.5 %collective-permute-start.9 = (f32[8,4,2,256]{3,2,1,0:T(2,128)S(1)}, f32[8,4,2,256]{3,2,1,0:T(2,128)S(1)}, u32[]{:S(2)}, u32[]{:S(2)}) collective-permute-start(f32[8,4,2,256]{3,2,1,0:T(2,128)S(1)} %get-tuple-element.36), channel_id=1, source_target_pairs={{2,0},{4,2},{6,4},{8,6},{10,8},{12,10},{14,12},{16,14},{18,16},{20... | collective-permute-start | bytes 196616 | tf_op jit(solution)/shard_map/ppermute | solution.py:43
  39.2 1.8 collective-permute-done.8
  43.3 4.5 %collective-permute-start.13 = (f32[8,4,2,256]{3,2,1,0:T(2,128)S(1)}, f32[8,4,2,256]{3,2,1,0:T(2,128)S(1)}, u32[]{:S(2)}, u32[]{:S(2)}) collective-permute-start(f32[8,4,2,256]{3,2,1,0:T(2,128)S(1)} %get-tuple-element.34), channel_id=1, source_target_pairs={{2,0},{4,2},{6,4},{8,6},{10,8},{12,10},{14,12},{16,14},{18,16},{20... | collective-permute-start | bytes 196616 | tf_op jit(solution)/shard_map/ppermute | solution.py:43
  47.8 1.9 collective-permute-done.12
  52.0 4.5 %collective-permute-start.15 = (f32[8,4,2,256]{3,2,1,0:T(2,128)S(1)}, f32[8,4,2,256]{3,2,1,0:T(2,128)S(1)}, u32[]{:S(2)}, u32[]{:S(2)}) collective-permute-start(f32[8,4,2,256]{3,2,1,0:T(2,128)S(1)} %get-tuple-element.32), channel_id=1, source_target_pairs={{2,0},{4,2},{6,4},{8,6},{10,8},{12,10},{14,12},{16,14},{18,16},{20... | collective-permute-start | bytes 196616 | tf_op jit(solution)/shard_map/ppermute | solution.py:43
  56.5 1.9 collective-permute-done.14
  60.5 8.6 %copy.38 = f32[8,4,32,256]{0,3,2,1:T(8,128)} copy(f32[8,4,32,256]{3,2,1,0:T(8,128)S(1)} %fusion.88) | data formatting | bytes 2097152 | tf_op jit(solution)/shard_map/sub | solution.py:99
  69.1 6.5 %gather_fusion = f32[256,8]{1,0:T(8,128)S(1)} fusion(f32[8,32768]{0,1:T(8,128)} %bitcast.42, s32[1024]{0:T(1024)S(1)} %pad_clamp_fusion), kind=kCustom, calls=%fused_computation | custom fusion | bytes 17408 | tf_op jit(solution)/shard_map/jit(_take)/gather | solution.py:116
  76.8 6.0 %all-to-all-start = ((f32[16,1,192]{2,1,0:T(1,128)}), f32[16,1,192]{2,1,0:T(1,128)S(1)}, u32[]{:S(2)}, u32[]{:S(2)}) async-start(f32[16,1,192]{2,1,0:T(1,128)} %reshape.116), calls=%async_computation | async-start | bytes 32768 | tf_op jit(solution)/shard_map/all_to_all | solution.py:121
  82.9 6.5 %all-to-all-done = f32[16,1,192]{2,1,0:T(1,128)S(1)} async-done(((f32[16,1,192]{2,1,0:T(1,128)}), f32[16,1,192]{2,1,0:T(1,128)S(1)}, u32[]{:S(2)}, u32[]{:S(2)}) %all-to-all-start) | async-done | bytes 12320 | tf_op jit(solution)/shard_map/all_to_all | solution.py:121
  90.8 9.1 %all_to_all.10 = f32[16,1,192]{2,1,0:T(1,128)S(1)} all-to-all(f32[16,1,192]{2,1,0:T(1,128)S(1)} %reshape.118), channel_id=1, replica_groups=mesh['field'=16,'probe'=2] {'field'}, dimensions={0} | all-to-all | bytes 24576 | tf_op jit(solution)/shard_map/all_to_all | solution.py:125
  101.2 8.2 %scatter_custom_fusion = f32[8,32768]{0,1:T(8,128)} fusion(s32[256]{0:T(256)S(1)} %bitcast.53, f32[256,8]{1,0:T(8,128)S(1)} %fusion.153, f32[]{:T(128)} %constant.12.clone.1), kind=kCustom, calls=%fused_computation.2 | custom fusion | flops 2048 | bytes 1048580 | tf_op jit(solution)/shard_map/scatter-add | solution.py:132
  109.4 9.8 %copy.42 = f32[8,4,32,256]{3,2,1,0:T(8,128)S(1)} copy(f32[8,4,32,256]{0,3,2,1:T(8,128)} %bitcast.39) | data formatting | bytes 2097152 | tf_op jit(solution)/shard_map/reshape | solution.py:133
  119.3 4.4 %collective-permute-start.17 = (f32[8,4,2,256]{3,2,1,0:T(2,128)S(1)}, f32[8,4,2,256]{3,2,1,0:T(2,128)S(1)}, u32[]{:S(2)}, u32[]{:S(2)}) collective-permute-start(f32[8,4,2,256]{3,2,1,0:T(2,128)S(1)} %get-tuple-element.30), channel_id=1, source_target_pairs={{2,0},{4,2},{6,4},{8,6},{10,8},{12,10},{14,12},{16,14},{18,16},{20... | collective-permute-start | bytes 196616 | tf_op jit(solution)/shard_map/ppermute | solution.py:43
  123.8 1.9 collective-permute-done.16
  128.5 4.5 %collective-permute-start.19 = (f32[8,4,2,256]{3,2,1,0:T(2,128)S(1)}, f32[8,4,2,256]{3,2,1,0:T(2,128)S(1)}, u32[]{:S(2)}, u32[]{:S(2)}) collective-permute-start(f32[8,4,2,256]{3,2,1,0:T(2,128)S(1)} %get-tuple-element.28), channel_id=1, source_target_pairs={{2,0},{4,2},{6,4},{8,6},{10,8},{12,10},{14,12},{16,14},{18,16},{20... | collective-permute-start | bytes 196616 | tf_op jit(solution)/shard_map/ppermute | solution.py:43
  133.0 1.9 collective-permute-done.18
  137.5 4.8 %collective-permute-start.21 = (f32[8,4,2,256]{3,2,1,0:T(2,128)S(1)}, f32[8,4,2,256]{3,2,1,0:T(2,128)S(1)}, u32[]{:S(2)}, u32[]{:S(2)}) collective-permute-start(f32[8,4,2,256]{3,2,1,0:T(2,128)S(1)} %get-tuple-element.26), channel_id=1, source_target_pairs={{2,0},{4,2},{6,4},{8,6},{10,8},{12,10},{14,12},{16,14},{18,16},{20... | collective-permute-start | bytes 196616 | tf_op jit(solution)/shard_map/ppermute | solution.py:43
  142.3 1.7 collective-permute-done.20
  147.0 4.5 %collective-permute-start.23 = (f32[8,4,1,256]{3,2,1,0:T(1,128)S(1)}, f32[8,4,1,256]{3,2,1,0:T(1,128)S(1)}, u32[]{:S(2)}, u32[]{:S(2)}) collective-permute-start(f32[8,4,1,256]{3,2,1,0:T(1,128)S(1)} %get-tuple-element.24), channel_id=1, source_target_pairs={{2,0},{4,2},{6,4},{8,6},{10,8},{12,10},{14,12},{16,14},{18,16},{20... | collective-permute-start | bytes 98312 | tf_op jit(solution)/shard_map/ppermute | solution.py:43
  151.5 2.0 collective-permute-start.30
  153.5 8.3 %psum.15 = f32[16,24]{1,0:T(8,128)S(1)} all-reduce(f32[16,24]{1,0:T(8,128)S(1)} %get-tuple-element.47), channel_id=1, replica_groups=mesh['field'=16,'probe'=2] {'probe'}, use_global_device_ids=true, to_apply=%region_4.5 | all-reduce | flops 384 | bytes 3072 | tf_op jit(solution)/shard_map/psum | solution.py:156
  162.6 4.4 %collective-permute-start.25 = (f32[8,4,1,256]{3,2,1,0:T(1,128)S(1)}, f32[8,4,1,256]{3,2,1,0:T(1,128)S(1)}, u32[]{:S(2)}, u32[]{:S(2)}) collective-permute-start(f32[8,4,1,256]{3,2,1,0:T(1,128)S(1)} %get-tuple-element.22), channel_id=1, source_target_pairs={{2,0},{4,2},{6,4},{8,6},{10,8},{12,10},{14,12},{16,14},{18,16},{20... | collective-permute-start | bytes 98312 | tf_op jit(solution)/shard_map/ppermute | solution.py:43
  169.6 4.4 %collective-permute-start.27 = (f32[8,4,1,256]{3,2,1,0:T(1,128)S(1)}, f32[8,4,1,256]{3,2,1,0:T(1,128)S(1)}, u32[]{:S(2)}, u32[]{:S(2)}) collective-permute-start(f32[8,4,1,256]{3,2,1,0:T(1,128)S(1)} %get-tuple-element.20), channel_id=1, source_target_pairs={{2,0},{4,2},{6,4},{8,6},{10,8},{12,10},{14,12},{16,14},{18,16},{20... | collective-permute-start | bytes 98312 | tf_op jit(solution)/shard_map/ppermute | solution.py:43
  176.5 4.4 %collective-permute-start.29 = (f32[8,4,1,256]{3,2,1,0:T(1,128)S(1)}, f32[8,4,1,256]{3,2,1,0:T(1,128)S(1)}, u32[]{:S(2)}, u32[]{:S(2)}) collective-permute-start(f32[8,4,1,256]{3,2,1,0:T(1,128)S(1)} %get-tuple-element.18), channel_id=1, source_target_pairs={{2,0},{4,2},{6,4},{8,6},{10,8},{12,10},{14,12},{16,14},{18,16},{20... | collective-permute-start | bytes 98312 | tf_op jit(solution)/shard_map/ppermute | solution.py:43
  182.2 2.3 %reshape_reshape_reshape.3 = bf16[16,32768]{1,0:T(8,128)(2,1)} reshape(bf16[2,1,8,4,32,256]{5,4,3,2,1,0:T(8,128)(2,1)} %reverse_select_fusion) | data formatting | bytes 2097152 | tf_op jit(solution)/shard_map/reshape;reshape;reshape | solution.py:149
  188.1 31.9 %psum.14 = f32[8,16]{1,0:T(8,128)S(1)} all-reduce(f32[8,16]{1,0:T(8,128)S(1)} %fusion.185), channel_id=1, replica_groups=mesh['field'=16,'probe'=2] {'field'}, use_global_device_ids=true, to_apply=%region_2.3 | all-reduce | flops 128 | bytes 1024 | tf_op jit(solution)/shard_map/psum | solution.py:154
  (136 shorter events, 40.4 us)
Async XLA Ops:
  2.9 10.1 %collective-permute-start = (f32[8,4,1,256]{3,2,1,0:T(1,128)S(1)}, f32[8,4,1,256]{3,2,1,0:T(1,128)S(1)}, u32[]{:S(2)}, u32[]{:S(2)}) collective-permute-start(f32[8,4,1,256]{3,2,1,0:T(1,128)S(1)} %get-tuple-element.43), channel_id=1, source_target_pairs={{0,2},{2,4},{4,6},{6,8},{8,10},{10,12},{12,14},{14,16},{16,18},{18... | collective-permute-start | bytes 98312 | tf_op jit(solution)/shard_map/ppermute | solution.py:42
  3.4 9.6 %collective-permute-start.1 = (f32[8,4,1,256]{3,2,1,0:T(1,128)S(1)}, f32[8,4,1,256]{3,2,1,0:T(1,128)S(1)}, u32[]{:S(2)}, u32[]{:S(2)}) collective-permute-start(f32[8,4,1,256]{3,2,1,0:T(1,128)S(1)} %get-tuple-element.44), channel_id=1, source_target_pairs={{2,0},{4,2},{6,4},{8,6},{10,8},{12,10},{14,12},{16,14},{18,16},{20... | collective-permute-start | bytes 98312 | tf_op jit(solution)/shard_map/ppermute | solution.py:43
  8.5 30.7 %collective-permute-start.10 = (f32[4,2,256]{2,1,0:T(2,128)S(1)}, f32[4,2,256]{2,1,0:T(2,128)S(1)}, u32[]{:S(2)}, u32[]{:S(2)}) collective-permute-start(f32[4,2,256]{2,1,0:T(2,128)S(1)} %get-tuple-element.45), channel_id=1, source_target_pairs={{0,2},{2,4},{4,6},{6,8},{8,10},{10,12},{12,14},{14,16},{16,18},{18... | collective-permute-start | bytes 24584 | tf_op jit(solution)/shard_map/ppermute | solution.py:42
  8.6 30.6 %collective-permute-start.11 = (f32[4,2,256]{2,1,0:T(2,128)S(1)}, f32[4,2,256]{2,1,0:T(2,128)S(1)}, u32[]{:S(2)}, u32[]{:S(2)}) collective-permute-start(f32[4,2,256]{2,1,0:T(2,128)S(1)} %get-tuple-element.46), channel_id=1, source_target_pairs={{2,0},{4,2},{6,4},{8,6},{10,8},{12,10},{14,12},{16,14},{18,16},{20... | collective-permute-start | bytes 24584 | tf_op jit(solution)/shard_map/ppermute | solution.py:43
  13.8 6.1 %collective-permute-start.2 = (f32[8,4,1,256]{3,2,1,0:T(1,128)S(1)}, f32[8,4,1,256]{3,2,1,0:T(1,128)S(1)}, u32[]{:S(2)}, u32[]{:S(2)}) collective-permute-start(f32[8,4,1,256]{3,2,1,0:T(1,128)S(1)} %get-tuple-element.41), channel_id=1, source_target_pairs={{0,2},{2,4},{4,6},{6,8},{8,10},{10,12},{12,14},{14,16},{16,18},{18... | collective-permute-start | bytes 98312 | tf_op jit(solution)/shard_map/ppermute | solution.py:42
  13.8 6.0 %collective-permute-start.3 = (f32[8,4,1,256]{3,2,1,0:T(1,128)S(1)}, f32[8,4,1,256]{3,2,1,0:T(1,128)S(1)}, u32[]{:S(2)}, u32[]{:S(2)}) collective-permute-start(f32[8,4,1,256]{3,2,1,0:T(1,128)S(1)} %get-tuple-element.42), channel_id=1, source_target_pairs={{2,0},{4,2},{6,4},{8,6},{10,8},{12,10},{14,12},{16,14},{18,16},{20... | collective-permute-start | bytes 98312 | tf_op jit(solution)/shard_map/ppermute | solution.py:43
  20.6 6.2 %collective-permute-start.4 = (f32[8,4,1,256]{3,2,1,0:T(1,128)S(1)}, f32[8,4,1,256]{3,2,1,0:T(1,128)S(1)}, u32[]{:S(2)}, u32[]{:S(2)}) collective-permute-start(f32[8,4,1,256]{3,2,1,0:T(1,128)S(1)} %get-tuple-element.39), channel_id=1, source_target_pairs={{0,2},{2,4},{4,6},{6,8},{8,10},{10,12},{12,14},{14,16},{16,18},{18... | collective-permute-start | bytes 98312 | tf_op jit(solution)/shard_map/ppermute | solution.py:42
  20.7 6.1 %collective-permute-start.5 = (f32[8,4,1,256]{3,2,1,0:T(1,128)S(1)}, f32[8,4,1,256]{3,2,1,0:T(1,128)S(1)}, u32[]{:S(2)}, u32[]{:S(2)}) collective-permute-start(f32[8,4,1,256]{3,2,1,0:T(1,128)S(1)} %get-tuple-element.40), channel_id=1, source_target_pairs={{2,0},{4,2},{6,4},{8,6},{10,8},{12,10},{14,12},{16,14},{18,16},{20... | collective-permute-start | bytes 98312 | tf_op jit(solution)/shard_map/ppermute | solution.py:43
  27.6 6.2 %collective-permute-start.6 = (f32[8,4,1,256]{3,2,1,0:T(1,128)S(1)}, f32[8,4,1,256]{3,2,1,0:T(1,128)S(1)}, u32[]{:S(2)}, u32[]{:S(2)}) collective-permute-start(f32[8,4,1,256]{3,2,1,0:T(1,128)S(1)} %get-tuple-element.37), channel_id=1, source_target_pairs={{0,2},{2,4},{4,6},{6,8},{8,10},{10,12},{12,14},{14,16},{16,18},{18... | collective-permute-start | bytes 98312 | tf_op jit(solution)/shard_map/ppermute | solution.py:42
  27.7 6.1 %collective-permute-start.7 = (f32[8,4,1,256]{3,2,1,0:T(1,128)S(1)}, f32[8,4,1,256]{3,2,1,0:T(1,128)S(1)}, u32[]{:S(2)}, u32[]{:S(2)}) collective-permute-start(f32[8,4,1,256]{3,2,1,0:T(1,128)S(1)} %get-tuple-element.38), channel_id=1, source_target_pairs={{2,0},{4,2},{6,4},{8,6},{10,8},{12,10},{14,12},{16,14},{18,16},{20... | collective-permute-start | bytes 98312 | tf_op jit(solution)/shard_map/ppermute | solution.py:43
  34.6 6.5 %collective-permute-start.8 = (f32[8,4,2,256]{3,2,1,0:T(2,128)S(1)}, f32[8,4,2,256]{3,2,1,0:T(2,128)S(1)}, u32[]{:S(2)}, u32[]{:S(2)}) collective-permute-start(f32[8,4,2,256]{3,2,1,0:T(2,128)S(1)} %get-tuple-element.35), channel_id=1, source_target_pairs={{0,2},{2,4},{4,6},{6,8},{8,10},{10,12},{12,14},{14,16},{16,18},{18... | collective-permute-start | bytes 196616 | tf_op jit(solution)/shard_map/ppermute | solution.py:42
  34.7 6.4 %collective-permute-start.9 = (f32[8,4,2,256]{3,2,1,0:T(2,128)S(1)}, f32[8,4,2,256]{3,2,1,0:T(2,128)S(1)}, u32[]{:S(2)}, u32[]{:S(2)}) collective-permute-start(f32[8,4,2,256]{3,2,1,0:T(2,128)S(1)} %get-tuple-element.36), channel_id=1, source_target_pairs={{2,0},{4,2},{6,4},{8,6},{10,8},{12,10},{14,12},{16,14},{18,16},{20... | collective-permute-start | bytes 196616 | tf_op jit(solution)/shard_map/ppermute | solution.py:43
  43.2 6.5 %collective-permute-start.12 = (f32[8,4,2,256]{3,2,1,0:T(2,128)S(1)}, f32[8,4,2,256]{3,2,1,0:T(2,128)S(1)}, u32[]{:S(2)}, u32[]{:S(2)}) collective-permute-start(f32[8,4,2,256]{3,2,1,0:T(2,128)S(1)} %get-tuple-element.33), channel_id=1, source_target_pairs={{0,2},{2,4},{4,6},{6,8},{8,10},{10,12},{12,14},{14,16},{16,18},{18... | collective-permute-start | bytes 196616 | tf_op jit(solution)/shard_map/ppermute | solution.py:42
  43.3 6.4 %collective-permute-start.13 = (f32[8,4,2,256]{3,2,1,0:T(2,128)S(1)}, f32[8,4,2,256]{3,2,1,0:T(2,128)S(1)}, u32[]{:S(2)}, u32[]{:S(2)}) collective-permute-start(f32[8,4,2,256]{3,2,1,0:T(2,128)S(1)} %get-tuple-element.34), channel_id=1, source_target_pairs={{2,0},{4,2},{6,4},{8,6},{10,8},{12,10},{14,12},{16,14},{18,16},{20... | collective-permute-start | bytes 196616 | tf_op jit(solution)/shard_map/ppermute | solution.py:43
  51.9 6.5 %collective-permute-start.14 = (f32[8,4,2,256]{3,2,1,0:T(2,128)S(1)}, f32[8,4,2,256]{3,2,1,0:T(2,128)S(1)}, u32[]{:S(2)}, u32[]{:S(2)}) collective-permute-start(f32[8,4,2,256]{3,2,1,0:T(2,128)S(1)} %get-tuple-element.31), channel_id=1, source_target_pairs={{0,2},{2,4},{4,6},{6,8},{8,10},{10,12},{12,14},{14,16},{16,18},{18... | collective-permute-start | bytes 196616 | tf_op jit(solution)/shard_map/ppermute | solution.py:42
  52.0 6.4 %collective-permute-start.15 = (f32[8,4,2,256]{3,2,1,0:T(2,128)S(1)}, f32[8,4,2,256]{3,2,1,0:T(2,128)S(1)}, u32[]{:S(2)}, u32[]{:S(2)}) collective-permute-start(f32[8,4,2,256]{3,2,1,0:T(2,128)S(1)} %get-tuple-element.32), channel_id=1, source_target_pairs={{2,0},{4,2},{6,4},{8,6},{10,8},{12,10},{14,12},{16,14},{18,16},{20... | collective-permute-start | bytes 196616 | tf_op jit(solution)/shard_map/ppermute | solution.py:43
  76.8 12.6 %all-to-all-start = ((f32[16,1,192]{2,1,0:T(1,128)}), f32[16,1,192]{2,1,0:T(1,128)S(1)}, u32[]{:S(2)}, u32[]{:S(2)}) async-start(f32[16,1,192]{2,1,0:T(1,128)} %reshape.116), calls=%async_computation | async-start | bytes 32768 | tf_op jit(solution)/shard_map/all_to_all | solution.py:121
  119.3 6.4 %collective-permute-start.16 = (f32[8,4,2,256]{3,2,1,0:T(2,128)S(1)}, f32[8,4,2,256]{3,2,1,0:T(2,128)S(1)}, u32[]{:S(2)}, u32[]{:S(2)}) collective-permute-start(f32[8,4,2,256]{3,2,1,0:T(2,128)S(1)} %get-tuple-element.29), channel_id=1, source_target_pairs={{0,2},{2,4},{4,6},{6,8},{8,10},{10,12},{12,14},{14,16},{16,18},{18... | collective-permute-start | bytes 196616 | tf_op jit(solution)/shard_map/ppermute | solution.py:42
  119.3 6.4 %collective-permute-start.17 = (f32[8,4,2,256]{3,2,1,0:T(2,128)S(1)}, f32[8,4,2,256]{3,2,1,0:T(2,128)S(1)}, u32[]{:S(2)}, u32[]{:S(2)}) collective-permute-start(f32[8,4,2,256]{3,2,1,0:T(2,128)S(1)} %get-tuple-element.30), channel_id=1, source_target_pairs={{2,0},{4,2},{6,4},{8,6},{10,8},{12,10},{14,12},{16,14},{18,16},{20... | collective-permute-start | bytes 196616 | tf_op jit(solution)/shard_map/ppermute | solution.py:43
  128.4 6.4 %collective-permute-start.18 = (f32[8,4,2,256]{3,2,1,0:T(2,128)S(1)}, f32[8,4,2,256]{3,2,1,0:T(2,128)S(1)}, u32[]{:S(2)}, u32[]{:S(2)}) collective-permute-start(f32[8,4,2,256]{3,2,1,0:T(2,128)S(1)} %get-tuple-element.27), channel_id=1, source_target_pairs={{0,2},{2,4},{4,6},{6,8},{8,10},{10,12},{12,14},{14,16},{16,18},{18... | collective-permute-start | bytes 196616 | tf_op jit(solution)/shard_map/ppermute | solution.py:42
  128.5 6.4 %collective-permute-start.19 = (f32[8,4,2,256]{3,2,1,0:T(2,128)S(1)}, f32[8,4,2,256]{3,2,1,0:T(2,128)S(1)}, u32[]{:S(2)}, u32[]{:S(2)}) collective-permute-start(f32[8,4,2,256]{3,2,1,0:T(2,128)S(1)} %get-tuple-element.28), channel_id=1, source_target_pairs={{2,0},{4,2},{6,4},{8,6},{10,8},{12,10},{14,12},{16,14},{18,16},{20... | collective-permute-start | bytes 196616 | tf_op jit(solution)/shard_map/ppermute | solution.py:43
  137.5 6.5 %collective-permute-start.20 = (f32[8,4,2,256]{3,2,1,0:T(2,128)S(1)}, f32[8,4,2,256]{3,2,1,0:T(2,128)S(1)}, u32[]{:S(2)}, u32[]{:S(2)}) collective-permute-start(f32[8,4,2,256]{3,2,1,0:T(2,128)S(1)} %get-tuple-element.25), channel_id=1, source_target_pairs={{0,2},{2,4},{4,6},{6,8},{8,10},{10,12},{12,14},{14,16},{16,18},{18... | collective-permute-start | bytes 196616 | tf_op jit(solution)/shard_map/ppermute | solution.py:42
  137.5 6.7 %collective-permute-start.21 = (f32[8,4,2,256]{3,2,1,0:T(2,128)S(1)}, f32[8,4,2,256]{3,2,1,0:T(2,128)S(1)}, u32[]{:S(2)}, u32[]{:S(2)}) collective-permute-start(f32[8,4,2,256]{3,2,1,0:T(2,128)S(1)} %get-tuple-element.26), channel_id=1, source_target_pairs={{2,0},{4,2},{6,4},{8,6},{10,8},{12,10},{14,12},{16,14},{18,16},{20... | collective-permute-start | bytes 196616 | tf_op jit(solution)/shard_map/ppermute | solution.py:43
  146.9 14.9 %collective-permute-start.22 = (f32[8,4,1,256]{3,2,1,0:T(1,128)S(1)}, f32[8,4,1,256]{3,2,1,0:T(1,128)S(1)}, u32[]{:S(2)}, u32[]{:S(2)}) collective-permute-start(f32[8,4,1,256]{3,2,1,0:T(1,128)S(1)} %get-tuple-element.23), channel_id=1, source_target_pairs={{0,2},{2,4},{4,6},{6,8},{8,10},{10,12},{12,14},{14,16},{16,18},{18... | collective-permute-start | bytes 98312 | tf_op jit(solution)/shard_map/ppermute | solution.py:42
  147.0 14.8 %collective-permute-start.23 = (f32[8,4,1,256]{3,2,1,0:T(1,128)S(1)}, f32[8,4,1,256]{3,2,1,0:T(1,128)S(1)}, u32[]{:S(2)}, u32[]{:S(2)}) collective-permute-start(f32[8,4,1,256]{3,2,1,0:T(1,128)S(1)} %get-tuple-element.24), channel_id=1, source_target_pairs={{2,0},{4,2},{6,4},{8,6},{10,8},{12,10},{14,12},{16,14},{18,16},{20... | collective-permute-start | bytes 98312 | tf_op jit(solution)/shard_map/ppermute | solution.py:43
  151.5 22.5 %collective-permute-start.30 = (bf16[1,8,4,32,256]{4,3,2,1,0:T(8,128)(2,1)S(1)}, bf16[1,8,4,32,256]{4,3,2,1,0:T(8,128)(2,1)S(1)}, u32[]{:S(2)}, u32[]{:S(2)}) collective-permute-start(bf16[1,8,4,32,256]{4,3,2,1,0:T(8,128)(2,1)S(1)} %bitcast.40), channel_id=1, source_target_pairs={{0,1},{1,0},{2,3},{3,2},{4,5},{5,4},{6,7},{7,6},{8,9},{9,8},{10,11... | collective-permute-start | bytes 1572872 | tf_op jit(solution)/shard_map/ppermute | solution.py:24
  162.5 6.2 %collective-permute-start.24 = (f32[8,4,1,256]{3,2,1,0:T(1,128)S(1)}, f32[8,4,1,256]{3,2,1,0:T(1,128)S(1)}, u32[]{:S(2)}, u32[]{:S(2)}) collective-permute-start(f32[8,4,1,256]{3,2,1,0:T(1,128)S(1)} %get-tuple-element.21), channel_id=1, source_target_pairs={{0,2},{2,4},{4,6},{6,8},{8,10},{10,12},{12,14},{14,16},{16,18},{18... | collective-permute-start | bytes 98312 | tf_op jit(solution)/shard_map/ppermute | solution.py:42
  162.6 6.1 %collective-permute-start.25 = (f32[8,4,1,256]{3,2,1,0:T(1,128)S(1)}, f32[8,4,1,256]{3,2,1,0:T(1,128)S(1)}, u32[]{:S(2)}, u32[]{:S(2)}) collective-permute-start(f32[8,4,1,256]{3,2,1,0:T(1,128)S(1)} %get-tuple-element.22), channel_id=1, source_target_pairs={{2,0},{4,2},{6,4},{8,6},{10,8},{12,10},{14,12},{16,14},{18,16},{20... | collective-permute-start | bytes 98312 | tf_op jit(solution)/shard_map/ppermute | solution.py:43
  169.5 6.2 %collective-permute-start.26 = (f32[8,4,1,256]{3,2,1,0:T(1,128)S(1)}, f32[8,4,1,256]{3,2,1,0:T(1,128)S(1)}, u32[]{:S(2)}, u32[]{:S(2)}) collective-permute-start(f32[8,4,1,256]{3,2,1,0:T(1,128)S(1)} %get-tuple-element.19), channel_id=1, source_target_pairs={{0,2},{2,4},{4,6},{6,8},{8,10},{10,12},{12,14},{14,16},{16,18},{18... | collective-permute-start | bytes 98312 | tf_op jit(solution)/shard_map/ppermute | solution.py:42
  169.6 6.1 %collective-permute-start.27 = (f32[8,4,1,256]{3,2,1,0:T(1,128)S(1)}, f32[8,4,1,256]{3,2,1,0:T(1,128)S(1)}, u32[]{:S(2)}, u32[]{:S(2)}) collective-permute-start(f32[8,4,1,256]{3,2,1,0:T(1,128)S(1)} %get-tuple-element.20), channel_id=1, source_target_pairs={{2,0},{4,2},{6,4},{8,6},{10,8},{12,10},{14,12},{16,14},{18,16},{20... | collective-permute-start | bytes 98312 | tf_op jit(solution)/shard_map/ppermute | solution.py:43
  176.5 8.1 %collective-permute-start.28 = (f32[8,4,1,256]{3,2,1,0:T(1,128)S(1)}, f32[8,4,1,256]{3,2,1,0:T(1,128)S(1)}, u32[]{:S(2)}, u32[]{:S(2)}) collective-permute-start(f32[8,4,1,256]{3,2,1,0:T(1,128)S(1)} %get-tuple-element.17), channel_id=1, source_target_pairs={{0,2},{2,4},{4,6},{6,8},{8,10},{10,12},{12,14},{14,16},{16,18},{18... | collective-permute-start | bytes 98312 | tf_op jit(solution)/shard_map/ppermute | solution.py:42
  176.5 8.0 %collective-permute-start.29 = (f32[8,4,1,256]{3,2,1,0:T(1,128)S(1)}, f32[8,4,1,256]{3,2,1,0:T(1,128)S(1)}, u32[]{:S(2)}, u32[]{:S(2)}) collective-permute-start(f32[8,4,1,256]{3,2,1,0:T(1,128)S(1)} %get-tuple-element.18), channel_id=1, source_target_pairs={{2,0},{4,2},{6,4},{8,6},{10,8},{12,10},{14,12},{16,14},{18,16},{20... | collective-permute-start | bytes 98312 | tf_op jit(solution)/shard_map/ppermute | solution.py:43
  (8 other events, 83.5 us)
